TPU v7x, 128 devices: a whole 4x4x4 slice. The times are simulated.
128 devices in a mesh: gx: 16 (over z, y), gy: 8 (over x, core).
Axes of the slice: x: 4, y: 4, z: 4, core: 2. Of those that a mesh axis runs over, the one named last changes fastest.
Arguments:
- jacobian: bfloat16 [16384, 192, 384], P(('gx', 'gy')), may hold values from -0.3125 to 0.3125
- grain_slots: int32 [16384, 64], P(('gx', 'gy')), may hold values from 0 to 18431, as said below
- block_count: int32 [128], P(('gx', 'gy')), may hold values from 1 to 128, as said below
- impulse_start: float32 [16384, 192], P(('gx', 'gy')), may hold values from -3 to 3
- velocity_bias: float32 [16384, 192], P(('gx', 'gy')), may hold values from -6 to 6
- friction: float32 [16384, 64], P(('gx', 'gy')), may hold values from 0.2 to 0.8
- free_velocity: float32 [6, 262144], P(None, ('gx', 'gy')), may hold values from -6 to 6
- inverse_mass: float32 [6, 262144], P(None, ('gx', 'gy')), may hold values from 0.5 to 4
Outputs:
- impulses: float32 [16384, 192], P(('gx', 'gy'))
- velocities: float32 [6, 262144], P(None, ('gx', 'gy'))
Inputs may be any that keep to these rules, and one draw needn't show every extreme that they name: `grain_slots`: A slot value s * 2048 + l names grain l of the device at offset (s // 3 - 1, s % 3 - 1) along (gx, gy) from the block's device (the device holding the block's row); that device always exists. A device's first block_count block slots are live, the rest are not; some device has all 128 live.
All inputs are finite; a program needn't handle non-finite values.
Results may differ from a plain program's by a relative error of at most 0.014.
Values may be sent and summed in bfloat16 or wider, within the bound.
A program may use at most 128 MiB of HBM per device.

v0:
```python
import math
import jax
import jax.numpy as jnp
from jax import lax
from jax.sharding import Mesh
from jax.sharding import PartitionSpec as P

CB = 64
GB = 64
ITERS = 3
GX_GY = ("gx_0", "gx_1", "gy_0", "gy_1")
GX = ("gx_0", "gx_1")
GY = ("gy_0", "gy_1")
epsilon = 1e-06


def with_halo(array, sides, width):
    for axis, dim in sides:
        size, length = (lax.axis_size(axis), array.shape[dim])
        up = [(i, (i + 1) % size) for i in range(size - 1)]
        down = [(j, i) for i, j in up]
        last = lax.slice_in_dim(array, length - width, length, axis=dim)
        leading = lax.slice_in_dim(array, 0, width, axis=dim)
        before = lax.ppermute(last, axis, up)
        after = lax.ppermute(leading, axis, down)
        array = jnp.concatenate([before, array, after], axis=dim)
    return array


def from_behind(block, axis, distance):
    devices = range(lax.axis_size(axis))
    route = [(i - distance, i) for i in devices if i - distance in devices]
    return lax.ppermute(block, axis, route)


def one_axis_at_a_time(array, axes):
    for axis in axes:
        array = lax.psum(array, axis)
    return array


def momentum_weights(iterations):
    momentum = 1.0
    weights = []
    for iteration in range(iterations):
        upcoming = (-momentum * momentum + momentum * math.sqrt(momentum * momentum + 4.0)) / 2.0
        weights.append(momentum * (1.0 - momentum) / (momentum * momentum + upcoming))
        momentum = upcoming
    return weights


def project_cone(target, friction):
    normal = target[:, :CB]
    tangent_one = target[:, CB : 2 * CB]
    tangent_two = target[:, 2 * CB :]
    tangent_norm = jnp.sqrt(tangent_one * tangent_one + tangent_two * tangent_two)
    inside = tangent_norm <= friction * normal
    opposite = friction * tangent_norm <= -normal
    cone_normal = (normal + friction * tangent_norm) / (1.0 + friction * friction)
    cone_ratio = friction * cone_normal / jnp.where(tangent_norm > 0, tangent_norm, 1.0)
    new_normal = jnp.where(inside, normal, jnp.where(opposite, 0.0, cone_normal))
    shrink = jnp.where(inside, 1.0, jnp.where(opposite, 0.0, cone_ratio))
    return jnp.concatenate([new_normal, tangent_one * shrink, tangent_two * shrink], axis=1)


def shards(
    jacobian,
    grain_slots,
    block_count,
    impulse_start,
    velocity_bias,
    friction,
    free_velocity,
    inverse_mass,
):
    blocks = jacobian.shape[0]
    grains = free_velocity.shape[1]
    live_mask = (jnp.arange(blocks, dtype=jnp.int32) < block_count[0]).astype(jnp.float32)[:, None]

    def forward(grain_field):
        nearby = with_halo(grain_field.reshape(6, 1, 1, grains), ((GX, 1), (GY, 2)), 1)
        nearby = nearby.reshape(6, 9 * grains)
        picked = jnp.take(nearby, grain_slots, axis=1)
        picked = jnp.transpose(picked, (1, 0, 2)).reshape(blocks, 6 * GB)
        return jnp.einsum("bij,bj->bi", jacobian, picked, preferred_element_type=jnp.float32)

    def backward(impulse_field):
        pushes = jnp.einsum(
            "bij,bi->bj", jacobian, impulse_field, preferred_element_type=jnp.float32
        )
        pushes = jnp.transpose(pushes.reshape(blocks, 6, GB), (1, 0, 2))
        nearby = jnp.zeros((6, 9 * grains), jnp.float32).at[:, grain_slots].add(pushes)
        nearby = nearby.reshape(6, 3, 3, grains)
        row_sums = nearby[:, :, 1]
        for step_y in (-1, 1):
            row_sums = row_sums + from_behind(
                nearby[:, :, step_y + 1].astype(jnp.bfloat16), GY, step_y
            ).astype(jnp.float32)
        summed = row_sums[:, 1]
        for step_x in (-1, 1):
            summed = summed + from_behind(row_sums[:, step_x + 1], GX, step_x)
        return summed

    constraint_bias = velocity_bias + forward(free_velocity.astype(jnp.bfloat16))
    extrapolated = impulse_start * live_mask
    previous = extrapolated
    current = extrapolated
    weights = momentum_weights(ITERS)
    for iteration in range(ITERS):
        pushed = backward(extrapolated.astype(jnp.bfloat16))
        moved = inverse_mass * pushed
        totals = lax.psum(
            jnp.stack([jnp.sum(extrapolated * extrapolated), jnp.sum(pushed * moved)]), GX_GY
        )
        size_total, energy_total = (totals[0], totals[1])
        gradient = (forward(moved.astype(jnp.bfloat16)) + constraint_bias) * live_mask
        step_size = size_total / (energy_total + epsilon)
        current = project_cone(extrapolated - step_size * gradient, friction) * live_mask
        extrapolated = current + weights[iteration] * (current - previous)
        previous = current
    final_push = backward(current.astype(jnp.bfloat16))
    return (current, free_velocity + inverse_mass * final_push)


def solution(mesh):
    finer = Mesh(mesh.devices.reshape(4, 4, 4, 2), ("gx_0", "gx_1", "gy_0", "gy_1"))
    placed = (
        P(GX_GY, None, None),
        P(GX_GY, None),
        P(GX_GY),
        P(GX_GY, None),
        P(GX_GY, None),
        P(GX_GY, None),
        P(None, GX_GY),
        P(None, GX_GY),
    )
    return jax.shard_map(
        shards,
        mesh=finer,
        in_specs=placed,
        out_specs=(P(GX_GY, None), P(None, GX_GY)),
        check_vma=False,
    )
```

profile of v0, /device:TPU:34, one launch (start us, length us, event | category | flops | bytes accessed | tf_op | source)
XLA Modules:
  0.0 789.8 jit_solution(12597441963960114974)
XLA Ops:
  1.5 4.5 collective-permute-start.9
  11.1 9.1 %fusion = f32[128,384]{1,0:T(8,128)S(1)} fusion(bf16[128,192,384]{2,1,0:T(8,128)(2,1)} %param.10, f32[128,192]{1,0:T(8,128)S(1)} %copy.120), kind=kLoop, calls=%fused_computation.16 | loop fusion | flops 28262400 | bytes 19169280
  20.4 4.5 copy.112
  24.9 48.5 %scatter_custom_fusion = f32[6,18432]{0,1:T(8,128)} fusion(s32[8192]{0:T(1024)S(1)} %reshape.145, f32[8192,6]{1,0:T(8,128)} %bitcast.184, f32[]{:T(128)} %constant.14.clone.1), kind=kCustom, calls=%fused_computation.30 | custom fusion | flops 49152 | bytes 442880 | tf_op jit(solution)/shard_map/scatter-add | solution.py:92
  73.4 5.6 copy.50
  83.5 3.2 collective-permute-start.11
  88.7 6.0 collective-permute-start.2
  96.8 3.5 copy.55
  100.2 24.8 %gather_fusion.1 = bf16[8192,6]{1,0:T(8,128)(2,1)S(1)} fusion(bf16[6,18432]{0,1:T(8,128)(2,1)} %bitcast.180, s32[8192]{0:T(1024)S(1)} %broadcast_clamp_fusion), kind=kCustom, calls=%fused_computation.1.clone | custom fusion | bytes 229376 | tf_op jit(solution)/shard_map/jit(_take)/gather | solution.py:83
  125.7 6.0 collective-permute-start.5
  137.3 65.9 %psum.21 = f32[2]{0:T(128)S(1)} all-reduce(f32[2]{0:T(128)S(1)} %pad_maximum_fusion.8), channel_id=1, replica_groups=mesh['gx_0'=4,'gx_1'=4,'gy_0'=4,'gy_1'=2] {'gx_0','gx_1','gy_0','gy_1'}, use_global_device_ids=true, to_apply=%region_3.4 | all-reduce | flops 2 | bytes 16 | tf_op jit(solution)/shard_map/psum | solution.py:112
  203.3 3.1 collective-permute-start.7
  212.4 3.5 copy.52
  215.9 24.8 %gather_fusion = bf16[8192,6]{1,0:T(8,128)(2,1)S(1)} fusion(bf16[6,18432]{0,1:T(8,128)(2,1)} %bitcast.181, s32[8192]{0:T(1024)S(1)} %broadcast_clamp_fusion), kind=kCustom, calls=%fused_computation.clone | custom fusion | bytes 229376 | tf_op jit(solution)/shard_map/jit(_take)/gather | solution.py:83
  243.4 29.2 %fusion.5 = (f32[128,192]{1,0:T(8,128)S(1)}, f32[128,192]{1,0:T(8,128)S(1)}) fusion(f32[128,384]{1,0:T(8,128)S(1)} %copy.122, bf16[128,192,384]{2,1,0:T(8,128)(2,1)} %param.10, f32[128,384]{1,0:T(8,128)S(1)} %copy.121), kind=kLoop, calls=%fused_computation.21 | loop fusion | flops 47136768 | bytes 19464192
  273.6 9.1 %fusion.1 = f32[128,384]{1,0:T(8,128)S(1)} fusion(bf16[128,192,384]{2,1,0:T(8,128)(2,1)} %param.10, f32[128,192]{1,0:T(8,128)S(1)} %copy.123), kind=kLoop, calls=%fused_computation.17 | loop fusion | flops 28262400 | bytes 19169280
  282.9 4.5 copy.113
  287.4 48.5 %scatter_custom_fusion.1 = f32[6,18432]{0,1:T(8,128)} fusion(s32[8192]{0:T(1024)S(1)} %reshape.145, f32[8192,6]{1,0:T(8,128)} %bitcast.185, f32[]{:T(128)} %constant.14.clone.1), kind=kCustom, calls=%fused_computation.28 | custom fusion | flops 49152 | bytes 442880 | tf_op jit(solution)/shard_map/scatter-add | solution.py:92
  335.9 5.6 copy.60
  345.9 3.6 collective-permute-done.13
  349.6 3.7 collective-permute-start.14
  355.8 5.8 collective-permute-done.15
  364.1 3.9 collective-permute-start.16
  369.4 61.6 %psum.22 = f32[2]{0:T(128)S(1)} all-reduce(f32[2]{0:T(128)S(1)} %pad_maximum_fusion.9), channel_id=1, replica_groups=mesh['gx_0'=4,'gx_1'=4,'gy_0'=4,'gy_1'=2] {'gx_0','gx_1','gy_0','gy_1'}, use_global_device_ids=true, to_apply=%region_7.9 | all-reduce | flops 2 | bytes 16 | tf_op jit(solution)/shard_map/psum | solution.py:112
  431.0 2.9 collective-permute-start.19
  439.9 3.5 copy.62
  443.4 24.8 %gather_fusion.2 = bf16[8192,6]{1,0:T(8,128)(2,1)S(1)} fusion(bf16[6,18432]{0,1:T(8,128)(2,1)} %bitcast.182, s32[8192]{0:T(1024)S(1)} %broadcast_clamp_fusion), kind=kCustom, calls=%fused_computation.2.clone | custom fusion | bytes 229376 | tf_op jit(solution)/shard_map/jit(_take)/gather | solution.py:83
  470.7 15.7 %fusion.6 = f32[128,192]{1,0:T(8,128)S(1)} fusion(f32[128,384]{1,0:T(8,128)S(1)} %copy.124, bf16[128,192,384]{2,1,0:T(8,128)(2,1)} %param.10), kind=kLoop, calls=%fused_computation.22 | loop fusion | flops 28286976 | bytes 19169280
  487.3 9.1 %fusion.2 = f32[128,384]{1,0:T(8,128)S(1)} fusion(bf16[128,192,384]{2,1,0:T(8,128)(2,1)} %param.10, f32[128,192]{1,0:T(8,128)S(1)} %copy.125), kind=kLoop, calls=%fused_computation.18 | loop fusion | flops 28262400 | bytes 19169280
  496.6 4.5 copy.114
  501.1 48.5 %scatter_custom_fusion.2 = f32[6,18432]{0,1:T(8,128)} fusion(s32[8192]{0:T(1024)S(1)} %reshape.145, f32[8192,6]{1,0:T(8,128)} %bitcast.186, f32[]{:T(128)} %constant.14.clone.1), kind=kCustom, calls=%fused_computation.26 | custom fusion | flops 49152 | bytes 442880 | tf_op jit(solution)/shard_map/scatter-add | solution.py:92
  549.6 5.6 copy.67
  559.6 3.5 collective-permute-done.21
  563.2 3.6 collective-permute-start.22
  569.4 5.7 collective-permute-done.23
  577.6 3.9 collective-permute-start.24
  582.9 61.4 %psum.23 = f32[2]{0:T(128)S(1)} all-reduce(f32[2]{0:T(128)S(1)} %pad_maximum_fusion.10), channel_id=1, replica_groups=mesh['gx_0'=4,'gx_1'=4,'gy_0'=4,'gy_1'=2] {'gx_0','gx_1','gy_0','gy_1'}, use_global_device_ids=true, to_apply=%region_11.13 | all-reduce | flops 2 | bytes 16 | tf_op jit(solution)/shard_map/psum | solution.py:112
  644.4 2.9 collective-permute-start.27
  653.3 3.5 copy.69
  656.8 24.8 %gather_fusion.3 = bf16[8192,6]{1,0:T(8,128)(2,1)S(1)} fusion(bf16[6,18432]{0,1:T(8,128)(2,1)} %bitcast.179, s32[8192]{0:T(1024)S(1)} %broadcast_clamp_fusion), kind=kCustom, calls=%fused_computation.3.clone | custom fusion | bytes 229376 | tf_op jit(solution)/shard_map/jit(_take)/gather | solution.py:83
  684.1 15.7 %fusion.7 = f32[128,192]{1,0:T(8,128)S(1)} fusion(f32[128,384]{1,0:T(8,128)S(1)} %copy.126, bf16[128,192,384]{2,1,0:T(8,128)(2,1)} %param.10), kind=kLoop, calls=%fused_computation.23 | loop fusion | flops 28286976 | bytes 19169280
  700.7 9.1 %fusion.3 = f32[128,384]{1,0:T(8,128)S(1)} fusion(bf16[128,192,384]{2,1,0:T(8,128)(2,1)} %param.10, f32[128,192]{1,0:T(8,128)S(1)} %copy.127), kind=kLoop, calls=%fused_computation.19 | loop fusion | flops 28262400 | bytes 19169280
  710.0 4.5 copy.115
  714.5 48.5 %scatter_custom_fusion.3 = f32[6,18432]{0,1:T(8,128)} fusion(s32[8192]{0:T(1024)S(1)} %reshape.145, f32[8192,6]{1,0:T(8,128)} %bitcast.183, f32[]{:T(128)} %constant.14.clone.1), kind=kCustom, calls=%fused_computation.24 | custom fusion | flops 49152 | bytes 442880 | tf_op jit(solution)/shard_map/scatter-add | solution.py:92
  763.0 5.6 copy.74
  773.0 3.5 collective-permute-done.29
  776.6 4.1 collective-permute-start.30
  782.8 6.2 collective-permute-done.31
  (140 shorter events, 73.7 us)
Async XLA Ops:
  1.5 82.0 %collective-permute-start.9 = (bf16[6,1,1,2048]{3,0,2,1:T(8,128)(2,1)S(1)}, bf16[6,1,1,2048]{3,0,2,1:T(8,128)(2,1)S(1)}, u32[]{:S(2)}, u32[]{:S(2)}) collective-permute-start(bf16[6,1,1,2048]{3,0,2,1:T(8,128)(2,1)S(1)} %convert_bitcast_fusion), channel_id=1, source_target_pairs={{8,0},{16,8},{24,16},{32,24},{40,32},{48,40},{56,48},{64,56},{72,6... | collective-permute-start | bytes 73736 | tf_op jit(solution)/shard_map/ppermute | solution.py:25
  5.9 77.5 %collective-permute-start.8 = (bf16[6,1,1,2048]{3,0,2,1:T(8,128)(2,1)S(1)}, bf16[6,1,1,2048]{3,0,2,1:T(8,128)(2,1)S(1)}, u32[]{:S(2)}, u32[]{:S(2)}) collective-permute-start(bf16[6,1,1,2048]{3,0,2,1:T(8,128)(2,1)S(1)} %convert_bitcast_fusion), channel_id=1, source_target_pairs={{0,8},{8,16},{16,24},{24,32},{32,40},{40,48},{48,56},{56,64},{64,7... | collective-permute-start | bytes 73736 | tf_op jit(solution)/shard_map/ppermute | solution.py:24
  24.9 58.6 %copy-start.4 = (s32[128,64]{0,1:T(8,128)S(1)}, s32[128,64]{0,1:T(8,128)}, u32[]{:S(2)}) copy-start(s32[128,64]{0,1:T(8,128)} %param.11) | copy-start | bytes 98308
  73.3 51.8 %copy-start = (f32[6,2048]{1,0:T(8,128)S(1)}, f32[6,2048]{1,0:T(8,128)}, u32[]{:S(2)}) copy-start(f32[6,2048]{1,0:T(8,128)} %param.17) | copy-start | bytes 147460
  79.1 9.5 %collective-permute-start = (bf16[6,3,2048]{2,0,1:T(8,128)(2,1)S(1)}, bf16[6,3,2048]{2,0,1:T(8,128)(2,1)S(1)}, u32[]{:S(2)}, u32[]{:S(2)}) collective-permute-start(bf16[6,3,2048]{2,0,1:T(8,128)(2,1)S(1)} %get-tuple-element.31), channel_id=1, source_target_pairs={{1,0},{2,1},{3,2},{4,3},{5,4},{6,5},{7,6},{9,8},{10,9},{11,10},{12... | collective-permute-start | bytes 221192 | tf_op jit(solution)/shard_map/ppermute | solution.py:33
  81.0 7.6 collective-permute-start.1
  83.5 13.1 %collective-permute-start.11 = (bf16[6,3,1,2048]{3,0,2,1:T(8,128)(2,1)S(1)}, bf16[6,3,1,2048]{3,0,2,1:T(8,128)(2,1)S(1)}, u32[]{:S(2)}, u32[]{:S(2)}) collective-permute-start(bf16[6,3,1,2048]{3,0,2,1:T(8,128)(2,1)S(1)} %pad_maximum_fusion.5), channel_id=1, source_target_pairs={{1,0},{2,1},{3,2},{4,3},{5,4},{6,5},{7,6},{9,8},{10,9},{11,10},{12... | collective-permute-start | bytes 221192 | tf_op jit(solution)/shard_map/ppermute | solution.py:25
  86.7 10.0 %collective-permute-start.10 = (bf16[6,3,1,2048]{3,0,2,1:T(8,128)(2,1)S(1)}, bf16[6,3,1,2048]{3,0,2,1:T(8,128)(2,1)S(1)}, u32[]{:S(2)}, u32[]{:S(2)}) collective-permute-start(bf16[6,3,1,2048]{3,0,2,1:T(8,128)(2,1)S(1)} %pad_maximum_fusion.5), channel_id=1, source_target_pairs={{0,1},{1,2},{2,3},{3,4},{4,5},{5,6},{6,7},{8,9},{9,10},{10,11},{11... | collective-permute-start | bytes 221192 | tf_op jit(solution)/shard_map/ppermute | solution.py:24
  88.7 36.4 %collective-permute-start.2 = (f32[6,2048]{1,0:T(8,128)S(1)}, f32[6,2048]{1,0:T(8,128)S(1)}, u32[]{:S(2)}, u32[]{:S(2)}) collective-permute-start(f32[6,2048]{1,0:T(8,128)S(1)} %get-tuple-element.39), channel_id=1, source_target_pairs={{8,0},{16,8},{24,16},{32,24},{40,32},{48,40},{56,48},{64,56},{72,6... | collective-permute-start | bytes 147464 | tf_op jit(solution)/shard_map/ppermute | solution.py:33
  94.7 30.4 %collective-permute-start.3 = (f32[6,2048]{1,0:T(8,128)S(1)}, f32[6,2048]{1,0:T(8,128)S(1)}, u32[]{:S(2)}, u32[]{:S(2)}) collective-permute-start(f32[6,2048]{1,0:T(8,128)S(1)} %get-tuple-element.40), channel_id=1, source_target_pairs={{0,8},{8,16},{16,24},{24,32},{32,40},{40,48},{48,56},{56,64},{64,7... | collective-permute-start | bytes 147464 | tf_op jit(solution)/shard_map/ppermute | solution.py:33
  125.7 77.5 %collective-permute-start.5 = (bf16[6,1,1,2048]{3,0,2,1:T(8,128)(2,1)S(1)}, bf16[6,1,1,2048]{3,0,2,1:T(8,128)(2,1)S(1)}, u32[]{:S(2)}, u32[]{:S(2)}) collective-permute-start(bf16[6,1,1,2048]{3,0,2,1:T(8,128)(2,1)S(1)} %get-tuple-element.24), channel_id=1, source_target_pairs={{8,0},{16,8},{24,16},{32,24},{40,32},{48,40},{56,48},{64,56},{72,6... | collective-permute-start | bytes 73736 | tf_op jit(solution)/shard_map/ppermute | solution.py:25
  131.8 71.5 %collective-permute-start.4 = (bf16[6,1,1,2048]{3,0,2,1:T(8,128)(2,1)S(1)}, bf16[6,1,1,2048]{3,0,2,1:T(8,128)(2,1)S(1)}, u32[]{:S(2)}, u32[]{:S(2)}) collective-permute-start(bf16[6,1,1,2048]{3,0,2,1:T(8,128)(2,1)S(1)} %get-tuple-element.24), channel_id=1, source_target_pairs={{0,8},{8,16},{16,24},{24,32},{32,40},{40,48},{48,56},{56,64},{64,7... | collective-permute-start | bytes 73736 | tf_op jit(solution)/shard_map/ppermute | solution.py:24
  203.3 7.4 collective-permute-start.7
  206.4 5.9 collective-permute-start.6
  243.3 29.4 %copy-start.1 = (f32[128,192]{0,1:T(8,128)S(1)}, f32[128,192]{0,1:T(8,128)}, u32[]{:S(2)}) copy-start(f32[128,192]{0,1:T(8,128)} %param.13) | copy-start | bytes 294916
  243.3 29.4 %copy-start.5 = (f32[128,192]{0,1:T(8,128)S(1)}, f32[128,192]{0,1:T(8,128)}, u32[]{:S(2)}) copy-start(f32[128,192]{0,1:T(8,128)} %param.14) | copy-start | bytes 294916
  243.4 29.5 %copy-start.2 = (f32[128,64]{0,1:T(8,128)S(1)}, f32[128,64]{0,1:T(8,128)}, u32[]{:S(2)}) copy-start(f32[128,64]{0,1:T(8,128)} %param.15) | copy-start | bytes 98308
  341.6 4.3 collective-permute-start.12
  343.6 5.9 collective-permute-start.13
  349.6 6.2 collective-permute-start.14
  353.3 8.3 %collective-permute-start.15 = (f32[6,2048]{1,0:T(8,128)S(1)}, f32[6,2048]{1,0:T(8,128)S(1)}, u32[]{:S(2)}, u32[]{:S(2)}) collective-permute-start(f32[6,2048]{1,0:T(8,128)S(1)} %get-tuple-element.38), channel_id=1, source_target_pairs={{0,8},{8,16},{16,24},{24,32},{32,40},{40,48},{48,56},{56,64},{64,7... | collective-permute-start | bytes 147464 | tf_op jit(solution)/shard_map/ppermute | solution.py:33
  362.2 68.8 %collective-permute-start.17 = (bf16[6,1,1,2048]{3,0,2,1:T(8,128)(2,1)S(1)}, bf16[6,1,1,2048]{3,0,2,1:T(8,128)(2,1)S(1)}, u32[]{:S(2)}, u32[]{:S(2)}) collective-permute-start(bf16[6,1,1,2048]{3,0,2,1:T(8,128)(2,1)S(1)} %get-tuple-element.22), channel_id=1, source_target_pairs={{8,0},{16,8},{24,16},{32,24},{40,32},{48,40},{56,48},{64,56},{72,6... | collective-permute-start | bytes 73736 | tf_op jit(solution)/shard_map/ppermute | solution.py:25
  364.1 66.9 %collective-permute-start.16 = (bf16[6,1,1,2048]{3,0,2,1:T(8,128)(2,1)S(1)}, bf16[6,1,1,2048]{3,0,2,1:T(8,128)(2,1)S(1)}, u32[]{:S(2)}, u32[]{:S(2)}) collective-permute-start(bf16[6,1,1,2048]{3,0,2,1:T(8,128)(2,1)S(1)} %get-tuple-element.22), channel_id=1, source_target_pairs={{0,8},{8,16},{16,24},{24,32},{32,40},{40,48},{48,56},{56,64},{64,7... | collective-permute-start | bytes 73736 | tf_op jit(solution)/shard_map/ppermute | solution.py:24
  431.0 6.8 collective-permute-start.19
  433.9 5.9 collective-permute-start.18
  555.3 4.3 collective-permute-start.20
  557.2 5.9 collective-permute-start.21
  563.2 6.2 collective-permute-start.22
  566.8 8.3 %collective-permute-start.23 = (f32[6,2048]{1,0:T(8,128)S(1)}, f32[6,2048]{1,0:T(8,128)S(1)}, u32[]{:S(2)}, u32[]{:S(2)}) collective-permute-start(f32[6,2048]{1,0:T(8,128)S(1)} %get-tuple-element.36), channel_id=1, source_target_pairs={{0,8},{8,16},{16,24},{24,32},{32,40},{40,48},{48,56},{56,64},{64,7... | collective-permute-start | bytes 147464 | tf_op jit(solution)/shard_map/ppermute | solution.py:33
  575.7 68.6 %collective-permute-start.25 = (bf16[6,1,1,2048]{3,0,2,1:T(8,128)(2,1)S(1)}, bf16[6,1,1,2048]{3,0,2,1:T(8,128)(2,1)S(1)}, u32[]{:S(2)}, u32[]{:S(2)}) collective-permute-start(bf16[6,1,1,2048]{3,0,2,1:T(8,128)(2,1)S(1)} %get-tuple-element.20), channel_id=1, source_target_pairs={{8,0},{16,8},{24,16},{32,24},{40,32},{48,40},{56,48},{64,56},{72,6... | collective-permute-start | bytes 73736 | tf_op jit(solution)/shard_map/ppermute | solution.py:25
  577.6 66.7 %collective-permute-start.24 = (bf16[6,1,1,2048]{3,0,2,1:T(8,128)(2,1)S(1)}, bf16[6,1,1,2048]{3,0,2,1:T(8,128)(2,1)S(1)}, u32[]{:S(2)}, u32[]{:S(2)}) collective-permute-start(bf16[6,1,1,2048]{3,0,2,1:T(8,128)(2,1)S(1)} %get-tuple-element.20), channel_id=1, source_target_pairs={{0,8},{8,16},{16,24},{24,32},{32,40},{40,48},{48,56},{56,64},{64,7... | collective-permute-start | bytes 73736 | tf_op jit(solution)/shard_map/ppermute | solution.py:24
  644.4 6.8 collective-permute-start.27
  647.3 5.9 collective-permute-start.26
  714.5 74.5 %copy-start.3 = (f32[6,2048]{1,0:T(8,128)S(1)}, f32[6,2048]{1,0:T(8,128)}, u32[]{:S(2)}) copy-start(f32[6,2048]{1,0:T(8,128)} %param.16) | copy-start | bytes 147460
  768.7 4.3 collective-permute-start.28
  770.6 5.9 collective-permute-start.29
  776.6 6.2 collective-permute-start.30
  780.7 8.3 %collective-permute-start.31 = (f32[6,2048]{1,0:T(8,128)S(1)}, f32[6,2048]{1,0:T(8,128)S(1)}, u32[]{:S(2)}, u32[]{:S(2)}) collective-permute-start(f32[6,2048]{1,0:T(8,128)S(1)} %get-tuple-element.34), channel_id=1, source_target_pairs={{0,8},{8,16},{16,24},{24,32},{32,40},{40,48},{48,56},{56,64},{64,7... | collective-permute-start | bytes 147464 | tf_op jit(solution)/shard_map/ppermute | solution.py:33
where the time goes:
time: 799 us; the launch traced here: 790 us
  other arithmetic  304 us (38%)
  blocking collectives  189 us (24%)
  local copies, waits for them, and re-layouts  167 us (21%)
  starting transfers between devices  89.1 us (11%)
  waiting for transfers between devices  35 us (4%)
    scatter-add x4, other arithmetic, backward(): jnp.zeros((6, 9 * grains), jnp.float32).at[:, grain_slots].add(pushes)  194 us
    psum x3, blocking collectives, shards(): lax.psum(jnp.stack([jnp.sum(extrapolated * extrapolated), jnp.sum(pushed...  189 us
    gather x8, local copies, waits for them, and re-layouts, forward(): picked = jnp.take(nearby, grain_slots, axis=1)  108 us
    unnamed x13, other arithmetic  97.8 us
    ppermute x16, starting transfers between devices, from_behind(): return lax.ppermute(block, axis, route)  42.9 us
    ppermute x16, waiting for transfers between devices, from_behind(): return lax.ppermute(block, axis, route)  29.1 us
    ppermute x8, starting transfers between devices, with_halo(): after = lax.ppermute(leading, axis, down)  26.4 us
    reshape x4, local copies, waits for them, and re-layouts, backward(): nearby = nearby.reshape(6, 3, 3, grains)  22.5 us
  transfers between devices with their start and end apart: 32, of which 12 were waited for; matrix products, arithmetic and copies ran while one was open for 14% of the time, Pallas kernels for 0%

commit v1 on v0

--- a/solution.py
+++ b/solution.py
@@ -109,8 +109,11 @@
     for iteration in range(ITERS):
         pushed = backward(extrapolated.astype(jnp.bfloat16))
         moved = inverse_mass * pushed
-        totals = lax.psum(
-            jnp.stack([jnp.sum(extrapolated * extrapolated), jnp.sum(pushed * moved)]), GX_GY
+        totals = jnp.sum(
+            lax.all_gather(
+                jnp.stack([jnp.sum(extrapolated * extrapolated), jnp.sum(pushed * moved)]), GX_GY
+            ),
+            axis=0,
         )
         size_total, energy_total = (totals[0], totals[1])
         gradient = (forward(moved.astype(jnp.bfloat16)) + constraint_bias) * live_mask

time: 799 us -> 805 us (level)
  starting transfers between devices: 89.1 us -> 101 us
    psum x3 -> x0, blocking collectives: 189 us -> none  [shards(): lax.psum(jnp.stack([jnp.sum(extrapolated * extrapolated), jnp.sum(pushed...]
    unnamed x0 -> x3, blocking collectives: none -> 186 us
    ppermute x8, starting transfers between devices: 26.4 us -> 36.5 us  [with_halo(): after = lax.ppermute(leading, axis, down)]
    unnamed x13 -> x16, other arithmetic: 97.8 us -> 102 us
  transfers between devices with their start and end apart: 32 -> 32, of which waited for: 12 -> 11; matrix products, arithmetic and copies ran while one was open for 14% -> 13% of each run, Pallas kernels for 0% -> 0%
where the time goes in v1:
time: 805 us; the launch traced here: 796 us
  other arithmetic  304 us (38%)
  blocking collectives  186 us (23%)
  local copies, waits for them, and re-layouts  167 us (21%)
  starting transfers between devices  101 us (13%)
  waiting for transfers between devices  31.7 us (4%)
    scatter-add x4, other arithmetic, backward(): jnp.zeros((6, 9 * grains), jnp.float32).at[:, grain_slots].add(pushes)  194 us
    unnamed x3, blocking collectives  186 us
    gather x8, local copies, waits for them, and re-layouts, forward(): picked = jnp.take(nearby, grain_slots, axis=1)  108 us
    unnamed x16, other arithmetic  102 us
    ppermute x16, starting transfers between devices, from_behind(): return lax.ppermute(block, axis, route)  46.4 us
    ppermute x8, starting transfers between devices, with_halo(): after = lax.ppermute(leading, axis, down)  36.5 us
    ppermute x16, waiting for transfers between devices, from_behind(): return lax.ppermute(block, axis, route)  31 us
    reshape x4, local copies, waits for them, and re-layouts, backward(): nearby = nearby.reshape(6, 3, 3, grains)  22.5 us
  transfers between devices with their start and end apart: 32, of which 11 were waited for; matrix products, arithmetic and copies ran while one was open for 13% of the time, Pallas kernels for 0%

profile of v1, /device:TPU:34, one launch (start us, length us, event | category | flops | bytes accessed | tf_op | source)
XLA Modules:
  0.0 795.5 jit_solution(5879586189488415738)
XLA Ops:
  1.5 3.5 collective-permute-start.8
  5.0 4.5 collective-permute-start.9
  11.7 9.1 %fusion = f32[128,384]{1,0:T(8,128)S(1)} fusion(bf16[128,192,384]{2,1,0:T(8,128)(2,1)} %param.10, f32[128,192]{1,0:T(8,128)S(1)} %copy.120), kind=kLoop, calls=%fused_computation.16 | loop fusion | flops 28262400 | bytes 19169280
  21.0 4.5 copy.112
  25.7 48.5 %scatter_custom_fusion = f32[6,18432]{0,1:T(8,128)} fusion(s32[8192]{0:T(1024)S(1)} %reshape.145, f32[8192,6]{1,0:T(8,128)} %bitcast.183, f32[]{:T(128)} %constant.14.clone.1), kind=kCustom, calls=%fused_computation.30 | custom fusion | flops 49152 | bytes 442880 | tf_op jit(solution)/shard_map/scatter-add | solution.py:92
  74.2 5.6 copy.50
  92.4 3.5 collective-permute-start.3
  96.0 3.5 copy.55
  99.4 24.8 %gather_fusion.1 = bf16[8192,6]{1,0:T(8,128)(2,1)S(1)} fusion(bf16[6,18432]{0,1:T(8,128)(2,1)} %bitcast.180, s32[8192]{0:T(1024)S(1)} %broadcast_clamp_fusion), kind=kCustom, calls=%fused_computation.1.clone | custom fusion | bytes 229376 | tf_op jit(solution)/shard_map/jit(_take)/gather | solution.py:83
  129.1 6.0 collective-permute-start.5
  136.6 63.2 %all-reduce = f32[256]{0:T(256)S(1)} all-reduce(f32[256]{0:T(256)S(1)} %maximum_dynamic-update-slice_fusion), channel_id=2, replica_groups=mesh['gx_0'=4,'gx_1'=4,'gy_0'=4,'gy_1'=2] {'gx_0','gx_1','gy_0','gy_1'}, use_global_device_ids=true, to_apply=%add | all-reduce | flops 256 | bytes 2048
  202.0 4.1 collective-permute-start.7
  211.6 24.8 %gather_fusion = bf16[8192,6]{1,0:T(8,128)(2,1)S(1)} fusion(bf16[6,18432]{0,1:T(8,128)(2,1)} %bitcast.181, s32[8192]{0:T(1024)S(1)} %broadcast_clamp_fusion), kind=kCustom, calls=%fused_computation.clone | custom fusion | bytes 229376 | tf_op jit(solution)/shard_map/jit(_take)/gather | solution.py:83
  239.1 29.2 %fusion.5 = (f32[128,192]{1,0:T(8,128)S(1)}, f32[128,192]{1,0:T(8,128)S(1)}) fusion(f32[128,384]{1,0:T(8,128)S(1)} %copy.122, bf16[128,192,384]{2,1,0:T(8,128)(2,1)} %param.10, f32[128,384]{1,0:T(8,128)S(1)} %copy.121), kind=kLoop, calls=%fused_computation.21 | loop fusion | flops 47136768 | bytes 19464192
  269.3 9.1 %fusion.1 = f32[128,384]{1,0:T(8,128)S(1)} fusion(bf16[128,192,384]{2,1,0:T(8,128)(2,1)} %param.10, f32[128,192]{1,0:T(8,128)S(1)} %copy.123), kind=kLoop, calls=%fused_computation.17 | loop fusion | flops 28262400 | bytes 19169280
  278.6 4.5 copy.113
  283.1 48.5 %scatter_custom_fusion.1 = f32[6,18432]{0,1:T(8,128)} fusion(s32[8192]{0:T(1024)S(1)} %reshape.145, f32[8192,6]{1,0:T(8,128)} %bitcast.185, f32[]{:T(128)} %constant.14.clone.1), kind=kCustom, calls=%fused_computation.28 | custom fusion | flops 49152 | bytes 442880 | tf_op jit(solution)/shard_map/scatter-add | solution.py:92
  331.6 5.6 copy.60
  337.3 3.5 collective-permute-start.12
  343.0 3.7 collective-permute-done.13
  346.8 5.0 collective-permute-start.14
  353.8 6.3 collective-permute-done.15
  362.7 6.0 collective-permute-start.17
  370.4 61.3 %all-reduce.1 = f32[256]{0:T(256)S(1)} all-reduce(f32[256]{0:T(256)S(1)} %maximum_dynamic-update-slice_fusion.1), channel_id=3, replica_groups=mesh['gx_0'=4,'gx_1'=4,'gy_0'=4,'gy_1'=2] {'gx_0','gx_1','gy_0','gy_1'}, use_global_device_ids=true, to_apply=%add.1 | all-reduce | flops 256 | bytes 2048
  433.8 3.6 collective-permute-start.19
  443.2 24.8 %gather_fusion.2 = bf16[8192,6]{1,0:T(8,128)(2,1)S(1)} fusion(bf16[6,18432]{0,1:T(8,128)(2,1)} %bitcast.182, s32[8192]{0:T(1024)S(1)} %broadcast_clamp_fusion), kind=kCustom, calls=%fused_computation.2.clone | custom fusion | bytes 229376 | tf_op jit(solution)/shard_map/jit(_take)/gather | solution.py:83
  470.5 15.7 %fusion.6 = f32[128,192]{1,0:T(8,128)S(1)} fusion(f32[128,384]{1,0:T(8,128)S(1)} %copy.124, bf16[128,192,384]{2,1,0:T(8,128)(2,1)} %param.10), kind=kLoop, calls=%fused_computation.22 | loop fusion | flops 28286976 | bytes 19169280
  487.1 9.1 %fusion.2 = f32[128,384]{1,0:T(8,128)S(1)} fusion(bf16[128,192,384]{2,1,0:T(8,128)(2,1)} %param.10, f32[128,192]{1,0:T(8,128)S(1)} %copy.125), kind=kLoop, calls=%fused_computation.18 | loop fusion | flops 28262400 | bytes 19169280
  496.4 4.5 copy.114
  500.9 48.5 %scatter_custom_fusion.2 = f32[6,18432]{0,1:T(8,128)} fusion(s32[8192]{0:T(1024)S(1)} %reshape.145, f32[8192,6]{1,0:T(8,128)} %bitcast.186, f32[]{:T(128)} %constant.14.clone.1), kind=kCustom, calls=%fused_computation.26 | custom fusion | flops 49152 | bytes 442880 | tf_op jit(solution)/shard_map/scatter-add | solution.py:92
  549.4 5.6 copy.67
  555.1 3.7 collective-permute-start.20
  561.0 3.7 collective-permute-done.21
  564.8 4.5 collective-permute-start.22
  571.2 6.3 collective-permute-done.23
  580.1 6.0 collective-permute-start.25
  587.6 61.4 %all-reduce.2 = f32[256]{0:T(256)S(1)} all-reduce(f32[256]{0:T(256)S(1)} %maximum_dynamic-update-slice_fusion.2), channel_id=4, replica_groups=mesh['gx_0'=4,'gx_1'=4,'gy_0'=4,'gy_1'=2] {'gx_0','gx_1','gy_0','gy_1'}, use_global_device_ids=true, to_apply=%add.2 | all-reduce | flops 256 | bytes 2048
  651.2 3.6 collective-permute-start.27
  660.5 24.8 %gather_fusion.3 = bf16[8192,6]{1,0:T(8,128)(2,1)S(1)} fusion(bf16[6,18432]{0,1:T(8,128)(2,1)} %bitcast.179, s32[8192]{0:T(1024)S(1)} %broadcast_clamp_fusion), kind=kCustom, calls=%fused_computation.3.clone | custom fusion | bytes 229376 | tf_op jit(solution)/shard_map/jit(_take)/gather | solution.py:83
  687.8 15.7 %fusion.7 = f32[128,192]{1,0:T(8,128)S(1)} fusion(f32[128,384]{1,0:T(8,128)S(1)} %copy.126, bf16[128,192,384]{2,1,0:T(8,128)(2,1)} %param.10), kind=kLoop, calls=%fused_computation.23 | loop fusion | flops 28286976 | bytes 19169280
  704.5 9.1 %fusion.3 = f32[128,384]{1,0:T(8,128)S(1)} fusion(bf16[128,192,384]{2,1,0:T(8,128)(2,1)} %param.10, f32[128,192]{1,0:T(8,128)S(1)} %copy.127), kind=kLoop, calls=%fused_computation.19 | loop fusion | flops 28262400 | bytes 19169280
  713.7 4.5 copy.115
  718.2 48.5 %scatter_custom_fusion.3 = f32[6,18432]{0,1:T(8,128)} fusion(s32[8192]{0:T(1024)S(1)} %reshape.145, f32[8192,6]{1,0:T(8,128)} %bitcast.184, f32[]{:T(128)} %constant.14.clone.1), kind=kCustom, calls=%fused_computation.24 | custom fusion | flops 49152 | bytes 442880 | tf_op jit(solution)/shard_map/scatter-add | solution.py:92
  766.7 5.6 copy.74
  772.4 3.7 collective-permute-start.28
  778.4 3.7 collective-permute-done.29
  782.2 4.2 collective-permute-start.30
  788.3 6.3 collective-permute-done.31
  (149 shorter events, 73.0 us)
Async XLA Ops:
  1.5 82.8 %collective-permute-start.8 = (bf16[6,1,1,2048]{3,0,2,1:T(8,128)(2,1)S(1)}, bf16[6,1,1,2048]{3,0,2,1:T(8,128)(2,1)S(1)}, u32[]{:S(2)}, u32[]{:S(2)}) collective-permute-start(bf16[6,1,1,2048]{3,0,2,1:T(8,128)(2,1)S(1)} %convert_bitcast_fusion), channel_id=1, source_target_pairs={{0,8},{8,16},{16,24},{24,32},{32,40},{40,48},{48,56},{56,64},{64,7... | collective-permute-start | bytes 73736 | tf_op jit(solution)/shard_map/ppermute | solution.py:24
  5.0 79.3 %collective-permute-start.9 = (bf16[6,1,1,2048]{3,0,2,1:T(8,128)(2,1)S(1)}, bf16[6,1,1,2048]{3,0,2,1:T(8,128)(2,1)S(1)}, u32[]{:S(2)}, u32[]{:S(2)}) collective-permute-start(bf16[6,1,1,2048]{3,0,2,1:T(8,128)(2,1)S(1)} %convert_bitcast_fusion), channel_id=1, source_target_pairs={{8,0},{16,8},{24,16},{32,24},{40,32},{48,40},{56,48},{64,56},{72,6... | collective-permute-start | bytes 73736 | tf_op jit(solution)/shard_map/ppermute | solution.py:25
  11.7 13.8 %copy-start.4 = (s32[128,64]{0,1:T(8,128)S(1)}, s32[128,64]{0,1:T(8,128)}, u32[]{:S(2)}) copy-start(s32[128,64]{0,1:T(8,128)} %param.11) | copy-start | bytes 98308
  74.2 52.4 %copy-start = (f32[6,2048]{1,0:T(8,128)S(1)}, f32[6,2048]{1,0:T(8,128)}, u32[]{:S(2)}) copy-start(f32[6,2048]{1,0:T(8,128)} %param.17) | copy-start | bytes 147460
  79.9 10.0 %collective-permute-start = (bf16[6,3,2048]{2,0,1:T(8,128)(2,1)S(1)}, bf16[6,3,2048]{2,0,1:T(8,128)(2,1)S(1)}, u32[]{:S(2)}, u32[]{:S(2)}) collective-permute-start(bf16[6,3,2048]{2,0,1:T(8,128)(2,1)S(1)} %get-tuple-element.31), channel_id=1, source_target_pairs={{1,0},{2,1},{3,2},{4,3},{5,4},{6,5},{7,6},{9,8},{10,9},{11,10},{12... | collective-permute-start | bytes 221192 | tf_op jit(solution)/shard_map/ppermute | solution.py:33
  81.8 8.1 %collective-permute-start.1 = (bf16[6,3,2048]{2,0,1:T(8,128)(2,1)S(1)}, bf16[6,3,2048]{2,0,1:T(8,128)(2,1)S(1)}, u32[]{:S(2)}, u32[]{:S(2)}) collective-permute-start(bf16[6,3,2048]{2,0,1:T(8,128)(2,1)S(1)} %get-tuple-element.32), channel_id=1, source_target_pairs={{0,1},{1,2},{2,3},{3,4},{4,5},{5,6},{6,7},{8,9},{9,10},{10,11},{11... | collective-permute-start | bytes 221192 | tf_op jit(solution)/shard_map/ppermute | solution.py:33
  84.3 11.5 %collective-permute-start.10 = (bf16[6,3,1,2048]{3,0,2,1:T(8,128)(2,1)S(1)}, bf16[6,3,1,2048]{3,0,2,1:T(8,128)(2,1)S(1)}, u32[]{:S(2)}, u32[]{:S(2)}) collective-permute-start(bf16[6,3,1,2048]{3,0,2,1:T(8,128)(2,1)S(1)} %pad_maximum_fusion.5), channel_id=1, source_target_pairs={{0,1},{1,2},{2,3},{3,4},{4,5},{5,6},{6,7},{8,9},{9,10},{10,11},{11... | collective-permute-start | bytes 221192 | tf_op jit(solution)/shard_map/ppermute | solution.py:24
  87.4 8.5 %collective-permute-start.11 = (bf16[6,3,1,2048]{3,0,2,1:T(8,128)(2,1)S(1)}, bf16[6,3,1,2048]{3,0,2,1:T(8,128)(2,1)S(1)}, u32[]{:S(2)}, u32[]{:S(2)}) collective-permute-start(bf16[6,3,1,2048]{3,0,2,1:T(8,128)(2,1)S(1)} %pad_maximum_fusion.5), channel_id=1, source_target_pairs={{1,0},{2,1},{3,2},{4,3},{5,4},{6,5},{7,6},{9,8},{10,9},{11,10},{12... | collective-permute-start | bytes 221192 | tf_op jit(solution)/shard_map/ppermute | solution.py:25
  90.0 36.5 %collective-permute-start.2 = (f32[6,2048]{1,0:T(8,128)S(1)}, f32[6,2048]{1,0:T(8,128)S(1)}, u32[]{:S(2)}, u32[]{:S(2)}) collective-permute-start(f32[6,2048]{1,0:T(8,128)S(1)} %get-tuple-element.39), channel_id=1, source_target_pairs={{8,0},{16,8},{24,16},{32,24},{40,32},{48,40},{56,48},{64,56},{72,6... | collective-permute-start | bytes 147464 | tf_op jit(solution)/shard_map/ppermute | solution.py:33
  92.4 34.2 %collective-permute-start.3 = (f32[6,2048]{1,0:T(8,128)S(1)}, f32[6,2048]{1,0:T(8,128)S(1)}, u32[]{:S(2)}, u32[]{:S(2)}) collective-permute-start(f32[6,2048]{1,0:T(8,128)S(1)} %get-tuple-element.40), channel_id=1, source_target_pairs={{0,8},{8,16},{16,24},{24,32},{32,40},{40,48},{48,56},{56,64},{64,7... | collective-permute-start | bytes 147464 | tf_op jit(solution)/shard_map/ppermute | solution.py:33
  127.2 72.8 %collective-permute-start.4 = (bf16[6,1,1,2048]{3,0,2,1:T(8,128)(2,1)S(1)}, bf16[6,1,1,2048]{3,0,2,1:T(8,128)(2,1)S(1)}, u32[]{:S(2)}, u32[]{:S(2)}) collective-permute-start(bf16[6,1,1,2048]{3,0,2,1:T(8,128)(2,1)S(1)} %get-tuple-element.24), channel_id=1, source_target_pairs={{0,8},{8,16},{16,24},{24,32},{32,40},{40,48},{48,56},{56,64},{64,7... | collective-permute-start | bytes 73736 | tf_op jit(solution)/shard_map/ppermute | solution.py:24
  129.1 70.9 %collective-permute-start.5 = (bf16[6,1,1,2048]{3,0,2,1:T(8,128)(2,1)S(1)}, bf16[6,1,1,2048]{3,0,2,1:T(8,128)(2,1)S(1)}, u32[]{:S(2)}, u32[]{:S(2)}) collective-permute-start(bf16[6,1,1,2048]{3,0,2,1:T(8,128)(2,1)S(1)} %get-tuple-element.24), channel_id=1, source_target_pairs={{8,0},{16,8},{24,16},{32,24},{40,32},{48,40},{56,48},{64,56},{72,6... | collective-permute-start | bytes 73736 | tf_op jit(solution)/shard_map/ppermute | solution.py:25
  200.1 7.9 collective-permute-start.6
  202.0 6.0 collective-permute-start.7
  239.0 29.4 %copy-start.1 = (f32[128,192]{0,1:T(8,128)S(1)}, f32[128,192]{0,1:T(8,128)}, u32[]{:S(2)}) copy-start(f32[128,192]{0,1:T(8,128)} %param.13) | copy-start | bytes 294916
  239.1 29.4 %copy-start.5 = (f32[128,192]{0,1:T(8,128)S(1)}, f32[128,192]{0,1:T(8,128)}, u32[]{:S(2)}) copy-start(f32[128,192]{0,1:T(8,128)} %param.14) | copy-start | bytes 294916
  239.1 29.5 %copy-start.2 = (f32[128,64]{0,1:T(8,128)S(1)}, f32[128,64]{0,1:T(8,128)}, u32[]{:S(2)}) copy-start(f32[128,64]{0,1:T(8,128)} %param.15) | copy-start | bytes 98308
  337.3 5.7 collective-permute-start.12
  340.9 5.9 collective-permute-start.13
  346.8 7.0 collective-permute-start.14
  351.9 8.3 %collective-permute-start.15 = (f32[6,2048]{1,0:T(8,128)S(1)}, f32[6,2048]{1,0:T(8,128)S(1)}, u32[]{:S(2)}, u32[]{:S(2)}) collective-permute-start(f32[6,2048]{1,0:T(8,128)S(1)} %get-tuple-element.38), channel_id=1, source_target_pairs={{0,8},{8,16},{16,24},{24,32},{32,40},{40,48},{48,56},{56,64},{64,7... | collective-permute-start | bytes 147464 | tf_op jit(solution)/shard_map/ppermute | solution.py:33
  360.8 71.0 %collective-permute-start.16 = (bf16[6,1,1,2048]{3,0,2,1:T(8,128)(2,1)S(1)}, bf16[6,1,1,2048]{3,0,2,1:T(8,128)(2,1)S(1)}, u32[]{:S(2)}, u32[]{:S(2)}) collective-permute-start(bf16[6,1,1,2048]{3,0,2,1:T(8,128)(2,1)S(1)} %get-tuple-element.22), channel_id=1, source_target_pairs={{0,8},{8,16},{16,24},{24,32},{32,40},{40,48},{48,56},{56,64},{64,7... | collective-permute-start | bytes 73736 | tf_op jit(solution)/shard_map/ppermute | solution.py:24
  362.7 69.1 %collective-permute-start.17 = (bf16[6,1,1,2048]{3,0,2,1:T(8,128)(2,1)S(1)}, bf16[6,1,1,2048]{3,0,2,1:T(8,128)(2,1)S(1)}, u32[]{:S(2)}, u32[]{:S(2)}) collective-permute-start(bf16[6,1,1,2048]{3,0,2,1:T(8,128)(2,1)S(1)} %get-tuple-element.22), channel_id=1, source_target_pairs={{8,0},{16,8},{24,16},{32,24},{40,32},{48,40},{56,48},{64,56},{72,6... | collective-permute-start | bytes 73736 | tf_op jit(solution)/shard_map/ppermute | solution.py:25
  431.9 7.5 collective-permute-start.18
  433.8 5.8 collective-permute-start.19
  555.1 5.9 collective-permute-start.20
  558.8 5.9 collective-permute-start.21
  564.8 6.4 collective-permute-start.22
  569.3 8.3 %collective-permute-start.23 = (f32[6,2048]{1,0:T(8,128)S(1)}, f32[6,2048]{1,0:T(8,128)S(1)}, u32[]{:S(2)}, u32[]{:S(2)}) collective-permute-start(f32[6,2048]{1,0:T(8,128)S(1)} %get-tuple-element.36), channel_id=1, source_target_pairs={{0,8},{8,16},{16,24},{24,32},{32,40},{40,48},{48,56},{56,64},{64,7... | collective-permute-start | bytes 147464 | tf_op jit(solution)/shard_map/ppermute | solution.py:33
  578.2 71.0 %collective-permute-start.24 = (bf16[6,1,1,2048]{3,0,2,1:T(8,128)(2,1)S(1)}, bf16[6,1,1,2048]{3,0,2,1:T(8,128)(2,1)S(1)}, u32[]{:S(2)}, u32[]{:S(2)}) collective-permute-start(bf16[6,1,1,2048]{3,0,2,1:T(8,128)(2,1)S(1)} %get-tuple-element.20), channel_id=1, source_target_pairs={{0,8},{8,16},{16,24},{24,32},{32,40},{40,48},{48,56},{56,64},{64,7... | collective-permute-start | bytes 73736 | tf_op jit(solution)/shard_map/ppermute | solution.py:24
  580.1 69.1 %collective-permute-start.25 = (bf16[6,1,1,2048]{3,0,2,1:T(8,128)(2,1)S(1)}, bf16[6,1,1,2048]{3,0,2,1:T(8,128)(2,1)S(1)}, u32[]{:S(2)}, u32[]{:S(2)}) collective-permute-start(bf16[6,1,1,2048]{3,0,2,1:T(8,128)(2,1)S(1)} %get-tuple-element.20), channel_id=1, source_target_pairs={{8,0},{16,8},{24,16},{32,24},{40,32},{48,40},{56,48},{64,56},{72,6... | collective-permute-start | bytes 73736 | tf_op jit(solution)/shard_map/ppermute | solution.py:25
  649.2 7.5 collective-permute-start.26
  651.2 5.8 collective-permute-start.27
  718.2 76.4 %copy-start.3 = (f32[6,2048]{1,0:T(8,128)S(1)}, f32[6,2048]{1,0:T(8,128)}, u32[]{:S(2)}) copy-start(f32[6,2048]{1,0:T(8,128)} %param.16) | copy-start | bytes 147460
  772.4 5.9 collective-permute-start.28
  776.2 5.9 collective-permute-start.29
  782.2 6.2 collective-permute-start.30
  786.4 8.3 %collective-permute-start.31 = (f32[6,2048]{1,0:T(8,128)S(1)}, f32[6,2048]{1,0:T(8,128)S(1)}, u32[]{:S(2)}, u32[]{:S(2)}) collective-permute-start(f32[6,2048]{1,0:T(8,128)S(1)} %get-tuple-element.34), channel_id=1, source_target_pairs={{0,8},{8,16},{16,24},{24,32},{32,40},{40,48},{48,56},{56,64},{64,7... | collective-permute-start | bytes 147464 | tf_op jit(solution)/shard_map/ppermute | solution.py:33
